TPU v7x, 32 devices: a whole 2x2x4 slice. The times are simulated.
32 devices in a mesh: grp: 4 (over x, core), ep: 8 (over z, y).
Axes of the slice: x: 2, y: 2, z: 4, core: 2. Of those that a mesh axis runs over, the one named last changes fastest.
Arguments:
- tokens: bfloat16 [32768, 512], P(('grp', 'ep')), may hold values from -6 to 6
- segments: int32 [128, 256], P(('grp', 'ep')), may hold values from 0 to 7, never falling along the last dimension, each value on 1 to 128 neighbouring positions
- patch_mask: int32 [128, 256], P(('grp', 'ep')), may hold values 0 or 1
- choices: int32 [32768, 2], P(('grp', 'ep')), may hold values from 0 to 7, all different within a row
- priority: int32 [32, 1024], P(('grp', 'ep')), may hold values from 0 to 1023, each once within a row
- first_gain: bfloat16 [512], P(('grp', 'ep')), may hold values from 0.5 to 1.5
- joint_weight: bfloat16 [512, 1536], P(('grp', 'ep')), may hold values from -0.25 to 0.25
- output_weight: bfloat16 [512, 512], P(('grp', 'ep')), may hold values from -1 to 1
- second_gain: bfloat16 [512], P(('grp', 'ep')), may hold values from 0.5 to 1.5
- router_weight: bfloat16 [512, 8], P(('grp', 'ep')), may hold values from -0.19921875 to 0.19921875
- expert_up: bfloat16 [8, 512, 2048], P('ep'), may hold values from -0.25 to 0.25
- expert_down: bfloat16 [8, 2048, 512], P('ep'), may hold values from -0.75 to 0.75
- out_grad: bfloat16 [32768, 512], P(('grp', 'ep')), may hold values from -6 to 6
Outputs:
- output: bfloat16 [32768, 512], P(('grp', 'ep'))
- tokens_grad: float32 [32768, 512], P(('grp', 'ep'))
- first_gain_grad: float32 [512], P(('grp', 'ep'))
- joint_weight_grad: float32 [512, 1536], P(('grp', 'ep'))
- output_weight_grad: float32 [512, 512], P(('grp', 'ep'))
- second_gain_grad: float32 [512], P(('grp', 'ep'))
- router_weight_grad: float32 [512, 8], P(('grp', 'ep'))
- expert_up_grad: float32 [8, 512, 2048], P('ep')
- expert_down_grad: float32 [8, 2048, 512], P('ep')
Inputs may be any that keep to these rules, and one draw needn't show every extreme that they name: `segments`: within a sequence the ids never fall. `choices`: a token's two experts differ. `priority`: each row holds every number below 1024 once.
All inputs are finite; a program needn't handle non-finite values. No bound on the sum of `patch_mask` on one device may be relied on, other than what follows from the above.
Results may differ from a plain program's by a relative error of at most 0.013.
Values may be sent and summed in bfloat16 or wider, within the bound.
A program may use at most 192 MiB of HBM per device.

v0:
```python
import jax
import jax.numpy as jnp
from jax import lax
from jax.sharding import PartitionSpec as P

HEADS = 8
EPSILON = 1e-06
NEGATIVE = -1e30


def normalize(values, gain):
    mean = jnp.mean(values, axis=-1, keepdims=True)
    centred = values - mean
    inverse = lax.rsqrt(jnp.mean(centred * centred, axis=-1, keepdims=True) + EPSILON)
    unit = centred * inverse
    return (unit * gain, unit, inverse)


def normalize_back(incoming, gain, unit, inverse):
    scaled = incoming * gain
    inner = (
        scaled
        - jnp.mean(scaled, axis=-1, keepdims=True)
        - unit * jnp.mean(scaled * unit, axis=-1, keepdims=True)
    )
    return (inverse * inner, jnp.sum(incoming * unit, axis=0))


def outer(left, right):
    return lax.dot_general(
        left, right, (((0,), (0,)), ((), ())), preferred_element_type=jnp.float32
    )


def times_t(left, right):
    return lax.dot_general(
        left, right, (((1,), (1,)), ((), ())), preferred_element_type=jnp.float32
    )


def gelu_slope(values):
    normal_cdf = 0.5 * (1.0 + lax.erf(values * 0.7071067811865476))
    density = jnp.exp(-0.5 * values * values) * 0.3989422804014327
    return normal_cdf + values * density


def route(picks, live, ranks, expert_count, capacity):
    row_count = picks.shape[0]
    labels = lax.broadcasted_iota(jnp.int32, (row_count, expert_count), 1)
    first = (picks[:, 0:1] == labels).astype(jnp.int32)
    second = (picks[:, 1:2] == labels).astype(jnp.int32)
    live_col = live[:, None]
    earlier = (ranks[None, :] < ranks[:, None]).astype(jnp.int32)
    first_live = first * live_col
    second_live = second * live_col
    place_one = jnp.sum(
        jnp.dot(earlier, first_live, preferred_element_type=jnp.int32) * first, axis=1
    )
    ahead = (
        jnp.dot(earlier, second_live, preferred_element_type=jnp.int32)
        + jnp.sum(first_live, axis=0)[None, :]
    )
    place_two = jnp.sum(ahead * second, axis=1)
    keep_one = (live > 0) & (place_one < capacity)
    keep_two = (live > 0) & (place_two < capacity)
    dummy = expert_count * capacity
    slot_one = jnp.where(keep_one, picks[:, 0] * capacity + place_one, dummy)
    slot_two = jnp.where(keep_two, picks[:, 1] * capacity + place_two, dummy)
    pick_one = (first * keep_one[:, None].astype(jnp.int32)).astype(jnp.float32)
    pick_two = (second * keep_two[:, None].astype(jnp.int32)).astype(jnp.float32)
    return (slot_one, slot_two, pick_one, pick_two)


def visible(group, live):
    rows = group.shape[0]
    index = lax.broadcasted_iota(jnp.int32, (rows, rows), 0)
    other = lax.broadcasted_iota(jnp.int32, (rows, rows), 1)
    return (group[:, None] == group[None, :]) & ((live[None, :] > 0) | (index == other))


def attend_forward(query, key, value, allowed, factor):
    scores = jnp.einsum("qhd,khd->hqk", query, key, preferred_element_type=jnp.float32) * factor
    masked = jnp.where(allowed[None], scores, NEGATIVE)
    top = jnp.max(masked, axis=-1, keepdims=True)
    weights = jnp.exp(masked - top)
    total = jnp.sum(weights, axis=-1, keepdims=True)
    probs = (weights / total).astype(jnp.bfloat16)
    mixed = jnp.einsum("hqk,khd->qhd", probs, value, preferred_element_type=jnp.float32)
    return (mixed, top + jnp.log(total))


def attend_backward(query, key, value, allowed, log_total, grad_mixed, factor):
    scores = jnp.einsum("qhd,khd->hqk", query, key, preferred_element_type=jnp.float32) * factor
    masked = jnp.where(allowed[None], scores, NEGATIVE)
    probs = jnp.exp(masked - log_total)
    grad_value = jnp.einsum(
        "hqk,qhd->khd", probs.astype(jnp.bfloat16), grad_mixed, preferred_element_type=jnp.float32
    )
    grad_probs = jnp.einsum("qhd,khd->hqk", grad_mixed, value, preferred_element_type=jnp.float32)
    delta = jnp.sum(probs * grad_probs, axis=-1, keepdims=True)
    grad_scores = (probs * (grad_probs - delta)).astype(jnp.bfloat16)
    grad_query = (
        jnp.einsum("hqk,khd->qhd", grad_scores, key, preferred_element_type=jnp.float32) * factor
    )
    grad_key = (
        jnp.einsum("hqk,qhd->khd", grad_scores, query, preferred_element_type=jnp.float32) * factor
    )
    return jnp.stack([grad_query, grad_key, grad_value], axis=1)


def per_device(
    tokens,
    segments,
    patch_mask,
    choices,
    priority,
    first_gain,
    joint_weight,
    output_weight,
    second_gain,
    router_weight,
    expert_up,
    expert_down,
    out_grad,
):
    row_count, width = tokens.shape
    head_size = width // HEADS
    factor = head_size ** (-0.5)
    expert_count = router_weight.shape[1]
    length = segments.shape[1]
    capacity = (21 * choices.shape[1] * row_count + 20 * expert_count - 1) // (20 * expert_count)
    block_rows = min(row_count, 512)
    gain_one, joint_full, output_full, gain_two, router_full = (
        lax.all_gather(first_gain, ("grp", "ep"), axis=0, tiled=True),
        lax.all_gather(joint_weight, ("grp", "ep"), axis=0, tiled=True),
        lax.all_gather(output_weight, ("grp", "ep"), axis=0, tiled=True),
        lax.all_gather(second_gain, ("grp", "ep"), axis=0, tiled=True),
        lax.all_gather(router_weight, ("grp", "ep"), axis=0, tiled=True),
    )
    inputs = tokens.astype(jnp.float32)
    gain_one = gain_one.astype(jnp.float32)
    gain_two = gain_two.astype(jnp.float32)
    normed_f, unit_one, inverse_one = normalize(inputs, gain_one)
    normed = normed_f.astype(jnp.bfloat16)
    joint = jnp.dot(normed, joint_full, preferred_element_type=jnp.float32).astype(jnp.bfloat16)
    joint = joint.reshape(row_count, 3, HEADS, head_size)
    live = patch_mask.reshape(row_count)
    position = lax.broadcasted_iota(jnp.int32, (row_count,), 0)
    group = position // length * length + segments.reshape(row_count)
    masks = []
    mixed_parts = []
    log_parts = []
    for start in range(0, row_count, block_rows):
        allowed = visible(group[start : start + block_rows], live[start : start + block_rows])
        block = joint[start : start + block_rows]
        mixed_block, log_total = attend_forward(
            block[:, 0], block[:, 1], block[:, 2], allowed, factor
        )
        masks.append(allowed)
        mixed_parts.append(mixed_block)
        log_parts.append(log_total)
    mixed = jnp.concatenate(mixed_parts, axis=0).reshape(row_count, width).astype(jnp.bfloat16)
    state = inputs + jnp.dot(mixed, output_full, preferred_element_type=jnp.float32)
    normed_two_f, unit_two, inverse_two = normalize(state, gain_two)
    normed_two = normed_two_f.astype(jnp.bfloat16)
    logits = jnp.dot(normed_two, router_full, preferred_element_type=jnp.float32)
    gate = jax.nn.softmax(logits, axis=-1)
    slot_one, slot_two, pick_one, pick_two = route(
        choices, live, priority.reshape(row_count), expert_count, capacity
    )
    gate_one = jnp.sum(gate * pick_one, axis=1)
    gate_two = jnp.sum(gate * pick_two, axis=1)
    empty = jnp.zeros((expert_count * capacity + 1, width), jnp.bfloat16)
    outgoing = empty.at[slot_one].add(normed_two).at[slot_two].add(normed_two)
    outgoing = outgoing[: expert_count * capacity].reshape(expert_count, capacity, width)
    arrived = lax.all_to_all(outgoing, "ep", split_axis=0, concat_axis=1, tiled=True)
    pre = jnp.einsum("erd,edf->erf", arrived, expert_up, preferred_element_type=jnp.float32)
    act = jax.nn.gelu(pre, approximate=False).astype(jnp.bfloat16)
    produced = jnp.einsum(
        "erf,efd->erd", act, expert_down, preferred_element_type=jnp.float32
    ).astype(jnp.bfloat16)
    returned = lax.all_to_all(produced, "ep", split_axis=1, concat_axis=0, tiled=True)
    zero_row = jnp.zeros((1, width), jnp.bfloat16)
    flat = jnp.concatenate([returned.reshape(expert_count * capacity, width), zero_row], axis=0)
    got_one = flat[slot_one].astype(jnp.float32)
    got_two = flat[slot_two].astype(jnp.float32)
    output = (state + gate_one[:, None] * got_one + gate_two[:, None] * got_two).astype(
        jnp.bfloat16
    )
    grad = out_grad.astype(jnp.float32)
    grad_gate = (
        pick_one * jnp.sum(grad * got_one, axis=1)[:, None]
        + pick_two * jnp.sum(grad * got_two, axis=1)[:, None]
    )
    grad_logits = (gate * (grad_gate - jnp.sum(gate * grad_gate, axis=1, keepdims=True))).astype(
        jnp.bfloat16
    )
    grad_router = outer(normed_two, grad_logits)
    grad_normed_two = times_t(grad_logits, router_full)
    weighted_one = (gate_one[:, None] * grad).astype(jnp.bfloat16)
    weighted_two = (gate_two[:, None] * grad).astype(jnp.bfloat16)
    grad_out_rows = empty.at[slot_one].add(weighted_one).at[slot_two].add(weighted_two)
    grad_out_rows = grad_out_rows[: expert_count * capacity].reshape(expert_count, capacity, width)
    grad_arrived = lax.all_to_all(grad_out_rows, "ep", split_axis=0, concat_axis=1, tiled=True)
    rows_now = lax.all_to_all(outgoing, "ep", split_axis=0, concat_axis=1, tiled=True)
    pre_now = jnp.einsum("erd,edf->erf", rows_now, expert_up, preferred_element_type=jnp.float32)
    act_now = jax.nn.gelu(pre_now, approximate=False).astype(jnp.bfloat16)
    grad_down = jnp.einsum(
        "erf,erd->efd", act_now, grad_arrived, preferred_element_type=jnp.float32
    )
    grad_act = jnp.einsum(
        "erd,efd->erf", grad_arrived, expert_down, preferred_element_type=jnp.float32
    )
    grad_pre = (grad_act * gelu_slope(pre_now)).astype(jnp.bfloat16)
    grad_up = jnp.einsum("erd,erf->edf", rows_now, grad_pre, preferred_element_type=jnp.float32)
    grad_rows = jnp.einsum(
        "erf,edf->erd", grad_pre, expert_up, preferred_element_type=jnp.float32
    ).astype(jnp.bfloat16)
    grad_back = lax.all_to_all(grad_rows, "ep", split_axis=1, concat_axis=0, tiled=True)
    flat_grad = jnp.concatenate(
        [grad_back.reshape(expert_count * capacity, width), zero_row], axis=0
    )
    grad_normed_two = (
        grad_normed_two
        + flat_grad[slot_one].astype(jnp.float32)
        + flat_grad[slot_two].astype(jnp.float32)
    )
    grad_state_in, grad_gain_two = normalize_back(grad_normed_two, gain_two, unit_two, inverse_two)
    grad_state = grad + grad_state_in
    grad_branch = grad_state.astype(jnp.bfloat16)
    grad_output_w = outer(mixed, grad_branch)
    grad_mixed = (
        times_t(grad_branch, output_full).astype(jnp.bfloat16).reshape(row_count, HEADS, head_size)
    )
    grad_parts = []
    for number, start in enumerate(range(0, row_count, block_rows)):
        block = joint[start : start + block_rows]
        grad_parts.append(
            attend_backward(
                block[:, 0],
                block[:, 1],
                block[:, 2],
                masks[number],
                log_parts[number],
                grad_mixed[start : start + block_rows],
                factor,
            )
        )
    grad_joint = (
        jnp.concatenate(grad_parts, axis=0).reshape(row_count, 3 * width).astype(jnp.bfloat16)
    )
    grad_joint_w = outer(normed, grad_joint)
    grad_normed = times_t(grad_joint, joint_full)
    grad_inputs_in, grad_gain_one = normalize_back(grad_normed, gain_one, unit_one, inverse_one)
    tokens_grad = grad_state + grad_inputs_in
    shares = (
        lax.psum_scatter(grad_gain_one, ("grp", "ep"), scatter_dimension=0, tiled=True),
        lax.psum_scatter(grad_joint_w, ("grp", "ep"), scatter_dimension=0, tiled=True),
        lax.psum_scatter(grad_output_w, ("grp", "ep"), scatter_dimension=0, tiled=True),
        lax.psum_scatter(grad_gain_two, ("grp", "ep"), scatter_dimension=0, tiled=True),
        lax.psum_scatter(grad_router, ("grp", "ep"), scatter_dimension=0, tiled=True),
    )
    grad_up, grad_down = (
        lax.psum(grad_up.astype(jnp.bfloat16), "grp").astype(jnp.float32),
        lax.psum(grad_down.astype(jnp.bfloat16), "grp").astype(jnp.float32),
    )
    return (
        output,
        tokens_grad,
        shares[0],
        shares[1],
        shares[2],
        shares[3],
        shares[4],
        grad_up,
        grad_down,
    )


def solution(mesh):
    in_specs = (
        P(("grp", "ep"), None),
        P(("grp", "ep"), None),
        P(("grp", "ep"), None),
        P(("grp", "ep"), None),
        P(("grp", "ep"), None),
        P(("grp", "ep")),
        P(("grp", "ep"), None),
        P(("grp", "ep"), None),
        P(("grp", "ep")),
        P(("grp", "ep"), None),
        P("ep", None, None),
        P("ep", None, None),
        P(("grp", "ep"), None),
    )
    out_specs = (
        P(("grp", "ep"), None),
        P(("grp", "ep"), None),
        P(("grp", "ep")),
        P(("grp", "ep"), None),
        P(("grp", "ep"), None),
        P(("grp", "ep")),
        P(("grp", "ep"), None),
        P("ep", None, None),
        P("ep", None, None),
    )
    return jax.shard_map(
        per_device, mesh=mesh, in_specs=in_specs, out_specs=out_specs, check_vma=False
    )
```

profile of v0, /device:TPU:0, one launch (start us, length us, event | category | flops | bytes accessed | tf_op | source)
XLA Modules:
  0.0 1114.1 jit_solution(8089762748541029859)
XLA Ops:
  11.2 42.1 %all-reduce.7 = (bf16[512]{0:T(512)(128)(2,1)S(1)}, bf16[512]{0:T(512)(128)(2,1)S(1)}) all-reduce(bf16[512]{0:T(512)(128)(2,1)S(1)} %dynamic-update-slice, bf16[512]{0:T(512)(128)(2,1)S(1)} %dynamic-update-slice.1), channel_id=1, replica_groups=mesh['grp'=4,'ep'=8] {'grp','ep'}, use_global_device_ids=true, to_apply=%add.2 | all-reduce | flops 1024 | bytes 4096
  65.6 74.1 %all_gather.17 = bf16[512,512]{1,0:T(8,128)(2,1)} all-gather(bf16[16,512]{1,0:T(8,128)(2,1)S(1)} %copy-done.51), channel_id=1, replica_groups=mesh['grp'=4,'ep'=8] {'grp','ep'}, dimensions={0}, use_global_device_ids=true | all-gather | bytes 540672 | tf_op jit(solution)/shard_map/all_gather | solution.py:136
  173.4 9.2 scatter_custom_fusion
  182.6 10.6 scatter_fusion
  196.4 3.6 reshape.421
  200.0 53.0 %all_to_all.16 = bf16[8,269,512]{2,1,0:T(8,128)(2,1)} all-to-all(bf16[8,269,512]{2,1,0:T(8,128)(2,1)} %reshape.421), channel_id=1, replica_groups=mesh['grp'=4,'ep'=8] {'ep'}, dimensions={0} | all-to-all | bytes 4407296 | tf_op jit(solution)/shard_map/all_to_all | solution.py:176
  253.0 3.6 reshape.422
  256.7 43.5 %fusion.2 = (bf16[2152,2048]{1,0:T(8,128)(2,1)S(1)}, f32[2152,2048]{1,0:T(8,128)}) fusion(bf16[2152,512]{1,0:T(8,128)(2,1)} %reshape.422, bf16[1,512,2048]{2,1,0:T(8,128)(2,1)S(1)} %copy-done), kind=kOutput, calls=%fused_computation.12 | convolution fusion | flops 4799545344 | bytes 30744576 | tf_op jit(solution)/shard_map/erd,edf->erf/dot_general | solution.py:177
  300.2 5.7 fusion.32
  305.9 16.4 %copy.139 = bf16[1,2152,512]{2,0,1:T(2,128)(2,1)} copy(bf16[1,2152,512]{2,1,0:T(8,128)(2,1)S(1)} %fusion.32) | data formatting | bytes 4407296 | tf_op jit(solution)/shard_map/convert_element_type | solution.py:181
  322.8 16.5 %reduce = bf16[2152,512]{1,0:T(8,128)(2,1)} reduce(bf16[2152,1,512]{2,1,0:T(2,128)(2,1)} %bitcast.160, bf16[]{:T(256)} %broadcast.495), dimensions={1}, to_apply=%bitcast.153.reduce_sub_computation | reduce | bytes 4407298
  339.4 3.8 reshape.505
  343.2 4.4 all-to-all-start.1
  349.1 102.5 %all-gather = bf16[32,16,8]{1,2,0:T(8,128)(2,1)S(1)} all-gather(bf16[1,16,8]{1,2,0:T(8,128)(2,1)S(1)} %bitcast.205), channel_id=1, replica_groups=mesh['grp'=4,'ep'=8] {'grp','ep'}, dimensions={0}, use_global_device_ids=true | all-gather | bytes 8448 | tf_op jit(solution)/shard_map/all_gather | solution.py:138
  453.4 7.9 reshape.506
  465.7 7.0 gather_fusion.1
  474.9 7.0 gather_fusion
  492.9 9.0 scatter_custom_fusion.2
  501.9 10.6 scatter_fusion.1
  515.6 3.6 reshape.426
  519.3 52.0 %all_to_all.17 = bf16[8,269,512]{2,1,0:T(8,128)(2,1)} all-to-all(bf16[8,269,512]{2,1,0:T(8,128)(2,1)} %reshape.426), channel_id=1, replica_groups=mesh['grp'=4,'ep'=8] {'ep'}, dimensions={0} | all-to-all | bytes 4407296 | tf_op jit(solution)/shard_map/all_to_all | solution.py:204
  571.3 3.6 reshape.427
  574.9 13.4 %fusion.8 = bf16[2152,2048]{1,0:T(8,128)(2,1)S(1)} fusion(f32[2152,2048]{1,0:T(8,128)} %get-tuple-element.87, bf16[2152,512]{1,0:T(8,128)(2,1)} %reshape.427, bf16[1,2048,512]{2,1,0:T(8,128)(2,1)} %param.24), kind=kOutput, calls=%fused_computation.18 | convolution fusion | flops 4557144064 | bytes 30744576 | tf_op jit(solution)/shard_map/erd,efd->erf/dot_general | solution.py:211
  588.3 5.3 fusion.33
  593.7 16.4 %copy.138 = bf16[1,2152,512]{2,0,1:T(2,128)(2,1)} copy(bf16[1,2152,512]{2,1,0:T(8,128)(2,1)S(1)} %fusion.33) | data formatting | bytes 4407296 | tf_op jit(solution)/shard_map/convert_element_type | solution.py:218
  610.1 16.1 %reduce.1 = bf16[2152,512]{1,0:T(8,128)(2,1)} reduce(bf16[2152,1,512]{2,1,0:T(2,128)(2,1)} %bitcast.161, bf16[]{:T(256)} %broadcast.495), dimensions={1}, to_apply=%bitcast.152.reduce_sub_computation | reduce | bytes 4407298
  626.2 3.9 reshape.507
  630.1 4.4 all-to-all-start.3
  637.0 9.8 fusion.35
  646.9 9.9 fusion.34
  656.8 26.4 %all-to-all-done.3 = bf16[8,2,68864]{2,1,0:T(2,128)(2,1)} async-done(((bf16[8,2,68864]{2,1,0:T(2,128)(2,1)}), bf16[8,2,68864]{2,1,0:T(2,128)(2,1)}, u32[]{:S(2)}, u32[]{:S(2)}) %all-to-all-start.3) | async-done | bytes 2203680 | tf_op jit(solution)/shard_map/all_to_all | solution.py:219
  683.2 7.9 reshape.508
  695.5 7.0 gather_fusion.2
  702.6 7.0 gather_fusion.3
  714.2 3.4 multiply_reduce_fusion.2
  732.9 5.6 multiply_reduce_fusion
  746.5 3.8 fusion.77
  750.2 4.8 fusion.84
  755.0 4.9 fusion.81
  762.2 3.5 fusion.117
  765.7 12.3 %reduce-scatter.10.cloned.1.call-done = f32[16,8]{1,0:T(8,128)} async-done(((f32[512,8]{1,0:T(8,128)}), f32[16,8]{1,0:T(8,128)}) %reduce-scatter.10.cloned.1.call-update) | async-done | bytes 528
  779.4 85.5 %all-reduce.11.cloned.1.call-done = (bf16[1,512,2048]{2,1,0:T(8,128)(2,1)}, bf16[1,2048,512]{2,1,0:T(8,128)(2,1)}) async-done(((bf16[1,512,2048]{2,1,0:T(8,128)(2,1)}, bf16[1,2048,512]{2,1,0:T(8,128)(2,1)}), (bf16[1,512,2048]{2,1,0:T(8,128)(2,1)}, bf16[1,2048,512]{2,1,0:T(8,128)(2,1)})) %all-reduce.11.cloned.1.call-update) | async-done | bytes 4194320 | tf_op jit(solution)/shard_map/psum | solution.py:264
  864.9 4.3 convert_element_type.178
  873.1 3.5 fusion.47
  876.5 39.7 %all-reduce.6 = (f32[512]{0:T(512)S(1)}, f32[512]{0:T(512)S(1)}) all-reduce(f32[512]{0:T(512)S(1)} %get-tuple-element.47, f32[512]{0:T(512)S(1)} %get-tuple-element.45), channel_id=2, replica_groups=mesh['grp'=4,'ep'=8] {'grp','ep'}, use_global_device_ids=true, to_apply=%region_29.30.clone | all-reduce | flops 1024 | bytes 8192
  917.4 4.2 fusion.46
  925.9 77.0 %reduce-scatter.8.cloned.1.call-done = f32[16,512]{1,0:T(8,128)} async-done(((f32[512,512]{1,0:T(8,128)}), f32[16,512]{1,0:T(8,128)}) %reduce-scatter.8.cloned.1.call-update) | async-done | bytes 32784 | tf_op jit(solution)/shard_map/reduce_scatter | solution.py:259
  1002.9 104.5 %reduce-scatter.6.cloned.1.call-done = f32[16,1536]{1,0:T(8,128)} async-done(((f32[512,1536]{1,0:T(8,128)}), f32[16,1536]{1,0:T(8,128)}) %reduce-scatter.6.cloned.1.call-update) | async-done | bytes 98320 | tf_op jit(solution)/shard_map/reduce_scatter | solution.py:258
  (245 shorter events, 124.5 us)
Async XLA Ops:
  7.2 249.5 %copy-start = (bf16[1,512,2048]{2,1,0:T(8,128)(2,1)S(1)}, bf16[1,512,2048]{2,1,0:T(8,128)(2,1)}, u32[]{:S(2)}) copy-start(bf16[1,512,2048]{2,1,0:T(8,128)(2,1)} %param.23) | copy-start | bytes 6291460
  7.2 57.0 %copy-start.46 = (s32[1024,2]{0,1:T(2,128)S(1)}, s32[1024,2]{0,1:T(2,128)}, u32[]{:S(2)}) copy-start(s32[1024,2]{0,1:T(2,128)} %param.16) | copy-start | bytes 24580
  7.2 58.4 %copy-start.51 = (bf16[16,512]{1,0:T(8,128)(2,1)S(1)}, bf16[16,512]{1,0:T(8,128)(2,1)}, u32[]{:S(2)}) copy-start(bf16[16,512]{1,0:T(8,128)(2,1)} %param.20) | copy-start | bytes 49156
  7.2 132.5 %all-gather.3.cloned.1.call-start = ((), (), s32[]{:S(2)}) async-start(), calls=%async_computation.7 | async-start | bytes 1622016 | tf_op jit(solution)/shard_map/all_gather | solution.py:135
  9.5 159.7 %copy-start.7 = (bf16[1024,512]{0,1:T(8,128)(2,1)}, bf16[1024,512]{0,1:T(8,128)(2,1)S(1)}, u32[]{:S(2)}) copy-start(bf16[1024,512]{0,1:T(8,128)(2,1)S(1)} %copy.92) | copy-start | bytes 3145732
  53.3 89.8 %copy-start.58 = (f32[512]{0:T(512)}, f32[512]{0:T(512)S(1)}, u32[]{:S(2)}) copy-start(f32[512]{0:T(512)S(1)} %convert_element_type.142) | copy-start | bytes 6148
  54.8 115.5 %copy-start.47 = (f32[512]{0:T(512)}, f32[512]{0:T(512)S(1)}, u32[]{:S(2)}) copy-start(f32[512]{0:T(512)S(1)} %convert_element_type.148) | copy-start | bytes 6148
  55.5 8.7 copy-start.42
  57.0 7.2 copy-start.38
  57.0 8.6 copy-start.44
  60.4 3.9 copy-start.54
  63.8 79.3 %copy-start.40 = (f32[1024]{0:T(1024)}, f32[1024]{0:T(1024)S(1)}, u32[]{:S(2)}) copy-start(f32[1024]{0:T(1024)S(1)} %broadcast_multiply_fusion.5) | copy-start | bytes 12292
  64.1 79.0 %copy-start.49 = (f32[1024]{0:T(1024)}, f32[1024]{0:T(1024)S(1)}, u32[]{:S(2)}) copy-start(f32[1024]{0:T(1024)S(1)} %add_rsqrt_fusion.1) | copy-start | bytes 12292
  64.2 109.2 %copy-start.52 = (s32[1024,1]{0,1:T(1,128)}, s32[1024,1]{0,1:T(1,128)S(1)}, u32[]{:S(2)}) copy-start(s32[1024,1]{0,1:T(1,128)S(1)} %get-tuple-element.73) | copy-start | bytes 12292
  172.1 21.1 %copy-start.9 = (bf16[1024,512]{0,1:T(8,128)(2,1)}, bf16[1024,512]{0,1:T(8,128)(2,1)S(1)}, u32[]{:S(2)}) copy-start(bf16[1024,512]{0,1:T(8,128)(2,1)S(1)} %multiply_convert_fusion.2) | copy-start | bytes 3145732
  256.7 43.5 %copy-start.61 = (bf16[1,2048,512]{2,1,0:T(8,128)(2,1)S(1)}, bf16[1,2048,512]{2,1,0:T(8,128)(2,1)}, u32[]{:S(2)}) copy-start(bf16[1,2048,512]{2,1,0:T(8,128)(2,1)} %param.24) | copy-start | bytes 6291460
  300.2 5.7 copy-start.64
  343.2 5.9 copy-start.60
  343.2 108.5 %copy-start.53 = (s32[1024,1]{0,1:T(1,128)S(1)}, s32[1024,1]{0,1:T(1,128)}, u32[]{:S(2)}) copy-start(s32[1024,1]{0,1:T(1,128)} %copy-done.52) | copy-start | bytes 12292
  343.2 108.6 %copy-start.43 = (s32[1,2,4,128]{3,1,2,0:T(2,128)S(1)}, s32[1,2,4,128]{3,1,2,0:T(2,128)}, u32[]{:S(2)}) copy-start(s32[1,2,4,128]{3,1,2,0:T(2,128)} %copy-done.42) | copy-start | bytes 12292
  343.2 108.6 %copy-start.55 = (s32[1024]{0:T(1024)S(1)}, s32[1024]{0:T(1024)}, u32[]{:S(2)}) copy-start(s32[1024]{0:T(1024)} %copy-done.54) | copy-start | bytes 12292
  343.2 108.6 %copy-start.57 = (s32[1024]{0:T(1024)S(1)}, s32[1024]{0:T(1024)}, u32[]{:S(2)}) copy-start(s32[1024]{0:T(1024)} %copy-done.56) | copy-start | bytes 12292
  343.2 110.1 %all-to-all-start.1 = ((bf16[8,2,68864]{2,1,0:T(2,128)(2,1)}), bf16[8,2,68864]{2,1,0:T(2,128)(2,1)}, u32[]{:S(2)}, u32[]{:S(2)}) async-start(bf16[8,2,68864]{2,1,0:T(2,128)(2,1)} %reshape.505), calls=%async_computation.1 | async-start | bytes 4407296 | tf_op jit(solution)/shard_map/all_to_all | solution.py:182
  482.0 4.4 copy-start.39
  482.0 4.5 copy-start.45
  588.3 5.3 copy-start.63
  626.2 8.4 copy-start.27
  626.2 8.4 copy-start.35
  626.2 8.4 copy-start.29
  626.2 8.4 copy-start.37
  630.1 53.2 %all-to-all-start.3 = ((bf16[8,2,68864]{2,1,0:T(2,128)(2,1)}), bf16[8,2,68864]{2,1,0:T(2,128)(2,1)}, u32[]{:S(2)}, u32[]{:S(2)}) async-start(bf16[8,2,68864]{2,1,0:T(2,128)(2,1)} %reshape.507), calls=%async_computation.3 | async-start | bytes 4407296 | tf_op jit(solution)/shard_map/all_to_all | solution.py:219
  634.5 143.6 %reduce-scatter.10.cloned.1.call-start = ((), (), s32[]{:S(2)}) async-start(), calls=%async_computation.10 | async-start | bytes 270336
  637.0 227.9 %all-reduce.11.cloned.1.call-start = ((), (), s32[]{:S(2)}) async-start(), calls=%async_computation.11 | async-start | bytes 8388608 | tf_op jit(solution)/shard_map/psum | solution.py:264
  637.0 9.8 copy-start.20
  656.8 346.1 %reduce-scatter.8.cloned.1.call-start = ((), (), s32[]{:S(2)}) async-start(), calls=%async_computation.9 | async-start | bytes 1081344 | tf_op jit(solution)/shard_map/reduce_scatter | solution.py:259
  709.6 4.6 copy-start.31
  709.6 4.6 copy-start.33
  709.6 4.6 copy-start.48
  717.7 4.7 slice-start.1
  720.0 11.2 %copy-start.6 = (f32[1024,512]{0,1:T(8,128)}, f32[1024,512]{0,1:T(8,128)S(1)}, u32[]{:S(2)}) copy-start(f32[1024,512]{0,1:T(8,128)S(1)} %get-tuple-element.66) | copy-start | bytes 6291460
  732.9 5.6 slice-start.2
  732.9 6.0 slice-start.3
  746.4 361.0 %reduce-scatter.6.cloned.1.call-start = ((), (), s32[]{:S(2)}) async-start(), calls=%async_computation.8 | async-start | bytes 3244032 | tf_op jit(solution)/shard_map/reduce_scatter | solution.py:258
  755.0 5.0 copy-start.22
  755.0 5.0 copy-start.23
  755.0 5.0 copy-start.24
  864.9 4.3 copy-start.21
  869.2 3.9 copy-start.62
  (28 other events, 70.6 us)
Sparse Core Ops, SparseCore 0:
  10.9 57.7 all-gather.2
  637.5 140.4 reduce-scatter.9
  781.2 83.6 all-reduce.10
  867.6 135.2 reduce-scatter.7
  1009.6 97.7 reduce-scatter.5
where the time goes:
time: 1120 us; the launch traced here: 1110 us
  blocking collectives  363 us (32%)
  waiting for transfers between devices  307 us (27%)
  local copies, waits for them, and re-layouts  164 us (15%)
  matrix products  154 us (14%)
  other arithmetic  102 us (9%)
  between operations  15 us (1%)
    reduce_scatter x1, waiting for transfers between devices, per_device(): lax.psum_scatter(grad_joint_w, ('grp', 'ep'), scatter_dimension=0, tiled=...  105 us
    all_gather x1, blocking collectives, per_device(): lax.all_gather(router_weight, ('grp', 'ep'), axis=0, tiled=True)  102 us
    psum x1, waiting for transfers between devices, per_device(): lax.psum(grad_up.astype(jnp.bfloat16), 'grp').astype(jnp.float32)  85.5 us
    unnamed x2, blocking collectives  81.8 us
    reduce_scatter x1, waiting for transfers between devices, per_device(): lax.psum_scatter(grad_output_w, ('grp', 'ep'), scatter_dimension=0, tiled...  77 us
    all_gather x1, blocking collectives, per_device(): lax.all_gather(output_weight, ('grp', 'ep'), axis=0, tiled=True)  74.1 us
    unnamed x160, local copies, waits for them, and re-layouts  56.1 us
    all_to_all x1, blocking collectives, per_device(): lax.all_to_all(outgoing, 'ep', split_axis=0, concat_axis=1, tiled=True)  53 us
  transfers between devices with their start and end apart: 7, of which 5 were waited for; matrix products, arithmetic and copies ran while one was open for 12% of the time, Pallas kernels for 0%

commit v1 on v0

--- a/solution.py
+++ b/solution.py
@@ -6,6 +6,28 @@
 HEADS = 8
 EPSILON = 1e-06
 NEGATIVE = -1e30
+
+
+def cut_along(x, dim, size):
+    before, after = (x.shape[:dim], x.shape[dim + 1 :])
+    return jnp.moveaxis(x.reshape(*before, size, -1, *after), dim, 0)
+
+
+def in_order(parts, dim):
+    parts = jnp.moveaxis(parts, 0, dim)
+    dims = parts.shape
+    return parts.reshape(*dims[:dim], dims[dim] * dims[dim + 1], *dims[dim + 2 :])
+
+
+def exchange_directly(x, axis, split_dim, concat_dim):
+    size, position = (lax.axis_size(axis), lax.axis_index(axis))
+    pieces = cut_along(x, split_dim, size)
+    done = [pieces[position]]
+    for turn in range(1, size):
+        sent = pieces[(position + turn) % size]
+        done.append(lax.ppermute(sent, axis, [(i, (i + turn) % size) for i in range(size)]))
+    pieces = jnp.stack(done)[(position - jnp.arange(size)) % size]
+    return in_order(pieces, concat_dim)
 
 
 def normalize(values, gain):
@@ -216,7 +238,7 @@
     grad_rows = jnp.einsum(
         "erf,edf->erd", grad_pre, expert_up, preferred_element_type=jnp.float32
     ).astype(jnp.bfloat16)
-    grad_back = lax.all_to_all(grad_rows, "ep", split_axis=1, concat_axis=0, tiled=True)
+    grad_back = exchange_directly(grad_rows, "ep", 1, 0)
     flat_grad = jnp.concatenate(
         [grad_back.reshape(expert_count * capacity, width), zero_row], axis=0
     )

time: 1120 us -> 1020 us (0.911)
  waiting for transfers between devices: 307 us -> 245 us
  blocking collectives: 363 us -> 328 us
  other arithmetic: 102 us -> 85.8 us
    psum x1, waiting for transfers between devices: 85.5 us -> 0.01 us  [per_device(): lax.psum(grad_up.astype(jnp.bfloat16), 'grp').astype(jnp.float32)]
    all_to_all x1 -> x0, blocking collectives: 52 us -> none  [per_device(): lax.all_to_all(grad_out_rows, 'ep', split_axis=0, concat_axis=1, tiled=True)]
    all_to_all x1, waiting for transfers between devices: 26.4 us -> 45.2 us  [per_device(): lax.all_to_all(grad_out_rows, 'ep', split_axis=0, concat_axis=1, tiled=True)]
    convert_element_type x1 -> x0, local copies, waits for them, and re-layouts: 16.4 us -> none  [per_device(): grad_rows = jnp.einsum('erf,edf->erd', grad_pre, expert_up, preferred_ele...]
    unnamed x2, blocking collectives: 81.8 us -> 98.2 us
    unnamed x5 -> x4, other arithmetic: 33.3 us -> 16.9 us
    ppermute x0 -> x7, waiting for transfers between devices: none -> 13.2 us  [exchange_directly(): lax.ppermute(sent, axis, [(i, (i + turn) % size) for i in range(size)])]
    unnamed x6, waiting for transfers between devices: 13.1 us -> 0.77 us
  transfers between devices with their start and end apart: 7 -> 14, of which waited for: 5 -> 5; matrix products, arithmetic and copies ran while one was open for 12% -> 17% of each run, Pallas kernels for 0% -> 0%
where the time goes in v1:
time: 1020 us; the launch traced here: 1010 us
  blocking collectives  328 us (32%)
  waiting for transfers between devices  245 us (24%)
  local copies, waits for them, and re-layouts  161 us (16%)
  matrix products  156 us (15%)
  other arithmetic  85.8 us (8%)
  starting transfers between devices  19.2 us (2%)
  between operations  15.1 us (1%)
    reduce_scatter x1, waiting for transfers between devices, per_device(): lax.psum_scatter(grad_joint_w, ('grp', 'ep'), scatter_dimension=0, tiled=...  104 us
    all_gather x1, blocking collectives, per_device(): lax.all_gather(router_weight, ('grp', 'ep'), axis=0, tiled=True)  102 us
    unnamed x2, blocking collectives  98.2 us
    reduce_scatter x1, waiting for transfers between devices, per_device(): lax.psum_scatter(grad_output_w, ('grp', 'ep'), scatter_dimension=0, tiled...  81.1 us
    all_gather x1, blocking collectives, per_device(): lax.all_gather(output_weight, ('grp', 'ep'), axis=0, tiled=True)  73.9 us
    all_to_all x1, blocking collectives, per_device(): lax.all_to_all(outgoing, 'ep', split_axis=0, concat_axis=1, tiled=True)  53.3 us
    unnamed x165, local copies, waits for them, and re-layouts  53 us
    all_to_all x1, waiting for transfers between devices, per_device(): lax.all_to_all(grad_out_rows, 'ep', split_axis=0, concat_axis=1, tiled=True)  45.2 us
  transfers between devices with their start and end apart: 14, of which 5 were waited for; matrix products, arithmetic and copies ran while one was open for 17% of the time, Pallas kernels for 0%

profile of v1, /device:TPU:0, one launch (start us, length us, event | category | flops | bytes accessed | tf_op | source)
XLA Modules:
  0.0 1009.2 jit_solution(15393945243241107567)
XLA Ops:
  11.2 42.1 %all-reduce.7 = (bf16[512]{0:T(512)(128)(2,1)S(1)}, bf16[512]{0:T(512)(128)(2,1)S(1)}) all-reduce(bf16[512]{0:T(512)(128)(2,1)S(1)} %dynamic-update-slice, bf16[512]{0:T(512)(128)(2,1)S(1)} %dynamic-update-slice.1), channel_id=1, replica_groups=mesh['grp'=4,'ep'=8] {'grp','ep'}, use_global_device_ids=true, to_apply=%add.2 | all-reduce | flops 1024 | bytes 4096
  64.9 73.9 %all_gather.17 = bf16[512,512]{1,0:T(8,128)(2,1)} all-gather(bf16[16,512]{1,0:T(8,128)(2,1)S(1)} %copy-done.51), channel_id=1, replica_groups=mesh['grp'=4,'ep'=8] {'grp','ep'}, dimensions={0}, use_global_device_ids=true | all-gather | bytes 540672 | tf_op jit(solution)/shard_map/all_gather | solution.py:158
  138.8 3.3 convolution_convert_fusion.2
  152.8 3.4 fusion.86
  172.1 9.2 scatter_custom_fusion
  181.3 10.6 %scatter_fusion = bf16[2153,512]{1,0:T(8,128)(2,1)} fusion(bf16[2153,512]{1,0:T(8,128)(2,1)} %scatter_custom_fusion, s32[1024]{0:T(1024)S(1)} %bitcast.202, bf16[1024,512]{1,0:T(8,128)(2,1)} %copy.97), kind=kCustom, calls=%fused_computation.6 | custom fusion | flops 524288 | bytes 3149824 | tf_op jit(solution)/shard_map/scatter-add | solution.py:196
  195.1 3.6 reshape.464
  198.7 53.3 %all_to_all.12 = bf16[8,269,512]{2,1,0:T(8,128)(2,1)} all-to-all(bf16[8,269,512]{2,1,0:T(8,128)(2,1)} %reshape.464), channel_id=1, replica_groups=mesh['grp'=4,'ep'=8] {'ep'}, dimensions={0} | all-to-all | bytes 4407296 | tf_op jit(solution)/shard_map/all_to_all | solution.py:198
  252.0 3.7 reshape.465
  255.7 43.6 %fusion.2 = (bf16[2152,2048]{1,0:T(8,128)(2,1)S(1)}, f32[2152,2048]{1,0:T(8,128)}) fusion(bf16[2152,512]{1,0:T(8,128)(2,1)} %reshape.465, bf16[1,512,2048]{2,1,0:T(8,128)(2,1)S(1)} %copy-done), kind=kOutput, calls=%fused_computation.13 | convolution fusion | flops 4799545344 | bytes 30744576 | tf_op jit(solution)/shard_map/erd,edf->erf/dot_general | solution.py:199
  299.3 5.7 fusion.32
  305.0 16.5 %copy.132 = bf16[1,2152,512]{2,0,1:T(2,128)(2,1)} copy(bf16[1,2152,512]{2,1,0:T(8,128)(2,1)S(1)} %fusion.32) | data formatting | bytes 4407296 | tf_op jit(solution)/shard_map/convert_element_type | solution.py:203
  322.0 16.2 %reduce = bf16[2152,512]{1,0:T(8,128)(2,1)} reduce(bf16[2152,1,512]{2,1,0:T(2,128)(2,1)} %bitcast.181, bf16[]{:T(256)} %broadcast.575), dimensions={1}, to_apply=%bitcast.175.reduce_sub_computation | reduce | bytes 4407298
  338.2 3.8 reshape.558
  342.0 4.4 all-to-all-start.1
  347.9 102.5 %all-gather = bf16[32,16,8]{1,2,0:T(8,128)(2,1)S(1)} all-gather(bf16[1,16,8]{1,2,0:T(8,128)(2,1)S(1)} %bitcast.225), channel_id=1, replica_groups=mesh['grp'=4,'ep'=8] {'grp','ep'}, dimensions={0}, use_global_device_ids=true | all-gather | bytes 8448 | tf_op jit(solution)/shard_map/all_gather | solution.py:160
  452.2 7.9 reshape.559
  464.5 7.0 gather_fusion.1
  473.8 7.0 gather_fusion
  491.7 9.0 scatter_custom_fusion.2
  500.7 11.0 %scatter_fusion.1 = bf16[2153,512]{1,0:T(8,128)(2,1)} fusion(bf16[2153,512]{1,0:T(8,128)(2,1)} %scatter_custom_fusion.2, s32[1024]{0:T(1024)S(1)} %bitcast.204, bf16[1024,512]{1,0:T(8,128)(2,1)} %copy.104), kind=kCustom, calls=%fused_computation.8 | custom fusion | flops 524288 | bytes 3149824 | tf_op jit(solution)/shard_map/scatter-add | solution.py:224
  514.8 3.6 reshape.469
  518.5 4.5 all-to-all-start.2
  525.7 45.2 %all-to-all-done.2 = bf16[8,269,512]{2,1,0:T(8,128)(2,1)} async-done(((bf16[8,269,512]{2,1,0:T(8,128)(2,1)}), bf16[8,269,512]{2,1,0:T(8,128)(2,1)}, u32[]{:S(2)}, u32[]{:S(2)}) %all-to-all-start.2) | async-done | bytes 2203680 | tf_op jit(solution)/shard_map/all_to_all | solution.py:226
  570.9 3.6 reshape.470
  574.6 9.3 fusion.34
  583.9 12.4 %fusion.8 = bf16[2152,2048]{1,0:T(8,128)(2,1)S(1)} fusion(f32[2152,2048]{1,0:T(8,128)} %get-tuple-element.95, bf16[2152,512]{1,0:T(8,128)(2,1)S(1)} %copy-done.20, bf16[1,2048,512]{2,1,0:T(8,128)(2,1)S(1)} %copy-done.62), kind=kOutput, calls=%fused_computation.19 | convolution fusion | flops 4557144064 | bytes 30744576 | tf_op jit(solution)/shard_map/erd,efd->erf/dot_general | solution.py:233
  596.4 3.4 copy-done.64
  599.8 6.2 convolution_convert_fusion
  606.0 3.6 transpose_reshape.3
  614.0 9.9 fusion.33
  635.9 10.8 %collective-permute-done.2 = bf16[1,269,512]{2,1,0:T(8,128)(2,1)} collective-permute-done((bf16[1,269,512]{2,1,0:T(8,128)(2,1)}, bf16[1,269,512]{2,1,0:T(8,128)(2,1)}, u32[]{:S(2)}, u32[]{:S(2)}) %collective-permute-start.2) | collective-permute-done | bytes 275488 | tf_op jit(solution)/shard_map/ppermute | solution.py:28
  655.6 3.7 gather_fusion.2
  659.3 3.6 reshape_reshape.3
  666.0 7.0 gather_fusion.3
  673.1 7.0 gather_fusion.4
  684.8 3.5 multiply_reduce_fusion.2
  703.7 5.6 multiply_reduce_fusion
  717.3 3.7 fusion.76
  721.0 5.3 fusion.83
  726.4 4.9 fusion.80
  733.5 3.5 fusion.116
  738.5 5.8 fusion.46
  744.3 56.1 %all-reduce.6 = (f32[512]{0:T(512)S(1)}, f32[512]{0:T(512)S(1)}) all-reduce(f32[512]{0:T(512)S(1)} %get-tuple-element.47, f32[512]{0:T(512)S(1)} %get-tuple-element.45), channel_id=2, replica_groups=mesh['grp'=4,'ep'=8] {'grp','ep'}, use_global_device_ids=true, to_apply=%region_29.30.clone | all-reduce | flops 1024 | bytes 8192
  801.5 4.2 fusion.45
  810.0 4.3 convert_element_type.175
  816.9 81.1 %reduce-scatter.8.cloned.1.call-done = f32[16,512]{1,0:T(8,128)} async-done(((f32[512,512]{1,0:T(8,128)}), f32[16,512]{1,0:T(8,128)}) %reduce-scatter.8.cloned.1.call-update) | async-done | bytes 32784 | tf_op jit(solution)/shard_map/reduce_scatter | solution.py:281
  898.0 104.5 %reduce-scatter.6.cloned.1.call-done = f32[16,1536]{1,0:T(8,128)} async-done(((f32[512,1536]{1,0:T(8,128)}), f32[16,1536]{1,0:T(8,128)}) %reduce-scatter.6.cloned.1.call-update) | async-done | bytes 98320 | tf_op jit(solution)/shard_map/reduce_scatter | solution.py:280
  (267 shorter events, 139.6 us)
Async XLA Ops:
  7.2 248.5 %copy-start = (bf16[1,512,2048]{2,1,0:T(8,128)(2,1)S(1)}, bf16[1,512,2048]{2,1,0:T(8,128)(2,1)}, u32[]{:S(2)}) copy-start(bf16[1,512,2048]{2,1,0:T(8,128)(2,1)} %param.23) | copy-start | bytes 6291460
  7.2 53.2 %copy-start.63 = (s32[1,1024]{1,0:T(1,128)S(1)}, s32[1,1024]{1,0:T(1,128)}, u32[]{:S(2)}) copy-start(s32[1,1024]{1,0:T(1,128)} %param.17) | copy-start | bytes 12292
  7.2 131.6 %all-gather.3.cloned.1.call-start = ((), (), s32[]{:S(2)}) async-start(), calls=%async_computation.6 | async-start | bytes 1622016 | tf_op jit(solution)/shard_map/all_gather | solution.py:157
  7.9 55.5 %copy-start.46 = (s32[1024,2]{0,1:T(2,128)S(1)}, s32[1024,2]{0,1:T(2,128)}, u32[]{:S(2)}) copy-start(s32[1024,2]{0,1:T(2,128)} %param.16) | copy-start | bytes 24580
  8.0 56.9 %copy-start.51 = (bf16[16,512]{1,0:T(8,128)(2,1)S(1)}, bf16[16,512]{1,0:T(8,128)(2,1)}, u32[]{:S(2)}) copy-start(bf16[16,512]{1,0:T(8,128)(2,1)} %param.20) | copy-start | bytes 49156
  9.5 158.3 %copy-start.7 = (bf16[1024,512]{0,1:T(8,128)(2,1)}, bf16[1024,512]{0,1:T(8,128)(2,1)S(1)}, u32[]{:S(2)}) copy-start(bf16[1024,512]{0,1:T(8,128)(2,1)S(1)} %copy.91) | copy-start | bytes 3145732
  53.3 88.8 %copy-start.58 = (f32[512]{0:T(512)}, f32[512]{0:T(512)S(1)}, u32[]{:S(2)}) copy-start(f32[512]{0:T(512)S(1)} %convert_element_type.140) | copy-start | bytes 6148
  54.8 114.1 %copy-start.47 = (f32[512]{0:T(512)}, f32[512]{0:T(512)S(1)}, u32[]{:S(2)}) copy-start(f32[512]{0:T(512)S(1)} %convert_element_type.146) | copy-start | bytes 6148
  55.5 8.0 copy-start.42
  57.0 6.5 copy-start.38
  57.0 7.9 copy-start.44
  63.1 79.1 %copy-start.40 = (f32[1024]{0:T(1024)}, f32[1024]{0:T(1024)S(1)}, u32[]{:S(2)}) copy-start(f32[1024]{0:T(1024)S(1)} %broadcast_multiply_fusion.5) | copy-start | bytes 12292
  63.4 78.7 %copy-start.49 = (f32[1024]{0:T(1024)}, f32[1024]{0:T(1024)S(1)}, u32[]{:S(2)}) copy-start(f32[1024]{0:T(1024)S(1)} %add_rsqrt_fusion.1) | copy-start | bytes 12292
  63.5 108.6 %copy-start.56 = (s32[1024,1]{0,1:T(1,128)}, s32[1024,1]{0,1:T(1,128)S(1)}, u32[]{:S(2)}) copy-start(s32[1024,1]{0,1:T(1,128)S(1)} %get-tuple-element.81) | copy-start | bytes 12292
  170.8 21.2 %copy-start.9 = (bf16[1024,512]{0,1:T(8,128)(2,1)}, bf16[1024,512]{0,1:T(8,128)(2,1)S(1)}, u32[]{:S(2)}) copy-start(bf16[1024,512]{0,1:T(8,128)(2,1)S(1)} %multiply_convert_fusion.2) | copy-start | bytes 3145732
  255.7 43.6 %copy-start.61 = (bf16[1,2048,512]{2,1,0:T(8,128)(2,1)S(1)}, bf16[1,2048,512]{2,1,0:T(8,128)(2,1)}, u32[]{:S(2)}) copy-start(bf16[1,2048,512]{2,1,0:T(8,128)(2,1)} %param.24) | copy-start | bytes 6291460
  299.3 5.7 copy-start.65
  342.0 5.9 copy-start.60
  342.0 108.5 %copy-start.43 = (s32[1,2,4,128]{3,1,2,0:T(2,128)S(1)}, s32[1,2,4,128]{3,1,2,0:T(2,128)}, u32[]{:S(2)}) copy-start(s32[1,2,4,128]{3,1,2,0:T(2,128)} %copy-done.42) | copy-start | bytes 12292
  342.0 108.5 %copy-start.53 = (s32[1024]{0:T(1024)S(1)}, s32[1024]{0:T(1024)}, u32[]{:S(2)}) copy-start(s32[1024]{0:T(1024)} %copy-done.52) | copy-start | bytes 12292
  342.0 108.6 %copy-start.55 = (s32[1024]{0:T(1024)S(1)}, s32[1024]{0:T(1024)}, u32[]{:S(2)}) copy-start(s32[1024]{0:T(1024)} %copy-done.54) | copy-start | bytes 12292
  342.0 108.6 %copy-start.57 = (s32[1024,1]{0,1:T(1,128)S(1)}, s32[1024,1]{0,1:T(1,128)}, u32[]{:S(2)}) copy-start(s32[1024,1]{0,1:T(1,128)} %copy-done.56) | copy-start | bytes 12292
  342.0 110.1 %all-to-all-start.1 = ((bf16[8,2,68864]{2,1,0:T(2,128)(2,1)}), bf16[8,2,68864]{2,1,0:T(2,128)(2,1)}, u32[]{:S(2)}, u32[]{:S(2)}) async-start(bf16[8,2,68864]{2,1,0:T(2,128)(2,1)} %reshape.558), calls=%async_computation.1 | async-start | bytes 4407296 | tf_op jit(solution)/shard_map/all_to_all | solution.py:204
  518.5 4.7 copy-start.27
  518.5 4.7 copy-start.35
  518.5 4.7 copy-start.29
  518.5 4.8 copy-start.37
  518.5 52.4 %all-to-all-start.2 = ((bf16[8,269,512]{2,1,0:T(8,128)(2,1)}), bf16[8,269,512]{2,1,0:T(8,128)(2,1)}, u32[]{:S(2)}, u32[]{:S(2)}) async-start(bf16[8,269,512]{2,1,0:T(8,128)(2,1)} %reshape.469), calls=%async_computation.2 | async-start | bytes 4456448 | tf_op jit(solution)/shard_map/all_to_all | solution.py:226
  523.0 214.1 %reduce-scatter.10.cloned.1.call-start = ((), (), s32[]{:S(2)}) async-start(), calls=%async_computation.9 | async-start | bytes 270336
  525.6 284.4 %all-reduce.11.cloned.1.call-start = ((), (), s32[]{:S(2)}) async-start(), calls=%async_computation.10 | async-start | bytes 8388608 | tf_op jit(solution)/shard_map/psum | solution.py:286
  574.6 9.3 copy-start.20
  574.6 9.3 copy-start.62
  612.6 17.3 %collective-permute-start = (bf16[1,269,512]{2,1,0:T(8,128)(2,1)}, bf16[1,269,512]{2,1,0:T(8,128)(2,1)}, u32[]{:S(2)}, u32[]{:S(2)}) collective-permute-start(bf16[1,269,512]{2,1,0:T(8,128)(2,1)} %get-tuple-element.72), channel_id=1, source_target_pairs={{0,1},{1,2},{2,3},{3,4},{4,5},{5,6},{6,7},{7,0},{8,9},{9,10},{10,1... | collective-permute-start | bytes 826376 | tf_op jit(solution)/shard_map/ppermute | solution.py:28
  613.9 19.5 %collective-permute-start.1 = (bf16[1,269,512]{2,1,0:T(8,128)(2,1)}, bf16[1,269,512]{2,1,0:T(8,128)(2,1)}, u32[]{:S(2)}, u32[]{:S(2)}) collective-permute-start(bf16[1,269,512]{2,1,0:T(8,128)(2,1)} %get-tuple-element.71), channel_id=1, source_target_pairs={{0,2},{1,3},{2,4},{3,5},{4,6},{5,7},{6,0},{7,1},{8,10},{9,11},{10,... | collective-permute-start | bytes 826376 | tf_op jit(solution)/shard_map/ppermute | solution.py:28
  624.0 22.7 %collective-permute-start.2 = (bf16[1,269,512]{2,1,0:T(8,128)(2,1)}, bf16[1,269,512]{2,1,0:T(8,128)(2,1)}, u32[]{:S(2)}, u32[]{:S(2)}) collective-permute-start(bf16[1,269,512]{2,1,0:T(8,128)(2,1)} %get-tuple-element.70), channel_id=1, source_target_pairs={{0,3},{1,4},{2,5},{3,6},{4,7},{5,0},{6,1},{7,2},{8,11},{9,12},{10,... | collective-permute-start | bytes 826376 | tf_op jit(solution)/shard_map/ppermute | solution.py:28
  626.2 24.5 %collective-permute-start.3 = (bf16[1,269,512]{2,1,0:T(8,128)(2,1)}, bf16[1,269,512]{2,1,0:T(8,128)(2,1)}, u32[]{:S(2)}, u32[]{:S(2)}) collective-permute-start(bf16[1,269,512]{2,1,0:T(8,128)(2,1)} %get-tuple-element.69), channel_id=1, source_target_pairs={{0,4},{1,5},{2,6},{3,7},{4,0},{5,1},{6,2},{7,3},{8,12},{9,13},{10,... | collective-permute-start | bytes 826376 | tf_op jit(solution)/shard_map/ppermute | solution.py:28
  628.0 24.4 %collective-permute-start.4 = (bf16[1,269,512]{2,1,0:T(8,128)(2,1)}, bf16[1,269,512]{2,1,0:T(8,128)(2,1)}, u32[]{:S(2)}, u32[]{:S(2)}) collective-permute-start(bf16[1,269,512]{2,1,0:T(8,128)(2,1)} %get-tuple-element.68), channel_id=1, source_target_pairs={{0,5},{1,6},{2,7},{3,0},{4,1},{5,2},{6,3},{7,4},{8,13},{9,14},{10,... | collective-permute-start | bytes 826376 | tf_op jit(solution)/shard_map/ppermute | solution.py:28
  629.8 268.2 %reduce-scatter.8.cloned.1.call-start = ((), (), s32[]{:S(2)}) async-start(), calls=%async_computation.8 | async-start | bytes 1081344 | tf_op jit(solution)/shard_map/reduce_scatter | solution.py:281
  629.9 24.2 %collective-permute-start.5 = (bf16[1,269,512]{2,1,0:T(8,128)(2,1)}, bf16[1,269,512]{2,1,0:T(8,128)(2,1)S(1)}, u32[]{:S(2)}, u32[]{:S(2)}) collective-permute-start(bf16[1,269,512]{2,1,0:T(8,128)(2,1)} %get-tuple-element.67), channel_id=1, source_target_pairs={{0,6},{1,7},{2,0},{3,1},{4,2},{5,3},{6,4},{7,5},{8,14},{9,15},{10,... | collective-permute-start | bytes 826376 | tf_op jit(solution)/shard_map/ppermute | solution.py:28
  633.4 21.5 %collective-permute-start.6 = (bf16[1,269,512]{2,1,0:T(8,128)(2,1)S(1)}, bf16[1,269,512]{2,1,0:T(8,128)(2,1)S(1)}, u32[]{:S(2)}, u32[]{:S(2)}) collective-permute-start(bf16[1,269,512]{2,1,0:T(8,128)(2,1)S(1)} %get-tuple-element.66), channel_id=1, source_target_pairs={{0,7},{1,0},{2,1},{3,2},{4,3},{5,4},{6,5},{7,6},{8,15},{9,8},{10,9... | collective-permute-start | bytes 826376 | tf_op jit(solution)/shard_map/ppermute | solution.py:28
  688.4 4.8 slice-start.1
  690.7 11.2 %copy-start.6 = (f32[1024,512]{0,1:T(8,128)}, f32[1024,512]{0,1:T(8,128)S(1)}, u32[]{:S(2)}) copy-start(f32[1024,512]{0,1:T(8,128)S(1)} %get-tuple-element.74) | copy-start | bytes 6291460
  703.7 5.6 slice-start.2
  703.7 6.1 slice-start.3
  717.0 285.4 %reduce-scatter.6.cloned.1.call-start = ((), (), s32[]{:S(2)}) async-start(), calls=%async_computation.7 | async-start | bytes 3244032 | tf_op jit(solution)/shard_map/reduce_scatter | solution.py:280
  726.4 5.0 copy-start.22
  726.4 5.0 copy-start.23
  726.4 5.0 copy-start.24
  (36 other events, 104.6 us)
Sparse Core Ops, SparseCore 0:
  10.9 57.8 all-gather.2
  526.1 147.3 reduce-scatter.9
  676.1 83.8 all-reduce.10
  762.7 135.2 reduce-scatter.7
  904.7 97.6 reduce-scatter.5
